TPU v7x, 32 devices: a whole 2x2x4 slice. The times are simulated.
32 devices in a mesh: tm: 8 (over z, x), space: 4 (over y, core).
Axes of the slice: x: 2, y: 2, z: 4, core: 2. Of those that a mesh axis runs over, the one named last changes fastest.
Arguments:
- snapshots: float32 [4224, 4096], P('tm', 'space')
- starts: int32 [32], replicated, may hold values from 0 to 3968, as said below
- freq_lines: int32 [128], replicated, may hold values from 0 to 128, as said below
Outputs:
- power_density: float32 [128, 4096], P(None, ('space', 'tm'))
- gram_matrices: float32 [2, 128, 32, 32], P(None, 'tm')
Inputs may be any that keep to these rules, and one draw needn't show every extreme that they name: starts never fall, and block b starts at most 64 snapshots away from b * 128; the first block starts at 0 and the last at 3968. `freq_lines`: distinct line numbers in any order; 0 and 128 are among them.
All inputs are finite; a program needn't handle non-finite values.
Results may differ from a plain program's by a relative error of at most 0.0001.
Values sent between devices are 32-bit elements; how exact they have to be, the bound alone decides.
No kernel may reach another device: no remote copies, remote signals or barrier semaphores. Data moves between devices by JAX's collectives and lax.ppermute only.
A program may use at most 64 MiB of HBM per device.

v0:
```python
import math
import jax
import jax.numpy as jnp
from jax import lax
from jax.sharding import PartitionSpec as P

NFFT = 256
NF = 128
NB = 32


def spectral_table(freq_lines):
    moments = jnp.arange(NFFT, dtype=jnp.int32)
    cycle = freq_lines[:, None] * moments[None, :] % NFFT
    angles = 2.0 * math.pi / NFFT * cycle.astype(jnp.float32)
    window = 0.5 - 0.5 * jnp.cos(2.0 * math.pi / NFFT * moments.astype(jnp.float32))
    window = window / jnp.sqrt(jnp.sum(window * window))
    return jnp.concatenate(
        [window[None, :] * jnp.cos(angles), -window[None, :] * jnp.sin(angles)], axis=0
    )


def block_spectra(series, starts, table):
    offsets = starts[:, None] + jnp.arange(NFFT, dtype=jnp.int32)[None, :]
    blocks = series[offsets]
    return jnp.einsum("kt,btp->kbp", table, blocks, precision=lax.Precision.HIGHEST)


def local_terms(spectra, factor):
    highest = lax.Precision.HIGHEST
    real_part = spectra[:NF]
    imag_part = spectra[NF:]
    power = jnp.sum(real_part * real_part + imag_part * imag_part, axis=1) / NB
    gram_real = jnp.einsum("fbp,fcp->fbc", real_part, real_part, precision=highest) + jnp.einsum(
        "fbp,fcp->fbc", imag_part, imag_part, precision=highest
    )
    gram_imag = jnp.einsum("fbp,fcp->fbc", real_part, imag_part, precision=highest) - jnp.einsum(
        "fbp,fcp->fbc", imag_part, real_part, precision=highest
    )
    return (power, jnp.stack([gram_real, gram_imag]) * factor)


def body(snapshots, starts, freq_lines):
    groups = lax.axis_size("tm")
    columns = snapshots.shape[1] // groups
    table = spectral_table(freq_lines)
    arranged = snapshots.reshape(snapshots.shape[0], groups, columns)
    spectra = block_spectra(
        lax.all_to_all(arranged, "tm", split_axis=1, concat_axis=0, tiled=True)[:, 0, :],
        starts,
        table,
    )
    total_points = columns * groups * lax.axis_size("space")
    power_density, own_gram = local_terms(spectra, 1.0 / (NB * total_points))
    per_device = NF // groups
    summed = lax.psum(own_gram, ("tm", "space"))
    gram_matrices = lax.dynamic_slice_in_dim(
        summed, lax.axis_index("tm") * per_device, per_device, 1
    )
    return (power_density, gram_matrices)


def solution(mesh):
    placed = (P("tm", "space"), P(), P())
    return jax.shard_map(
        body,
        mesh=mesh,
        in_specs=placed,
        out_specs=(P(None, ("space", "tm")), P(None, "tm", None, None)),
        check_vma=False,
    )
```

profile of v0, /device:TPU:0, one launch (start us, length us, event | category | flops | bytes accessed | tf_op | source)
XLA Modules:
  0.0 276.6 jit_solution(2760193698736418181)
XLA Ops:
  7.2 0.0 copy-start
  7.2 1.6 copy-done
  8.8 1.5 copy_bitcast_fusion
  10.3 0.0 copy-start.2
  10.3 0.0 copy-start.3
  10.3 7.4 %all-to-all-start = ((f32[528,8,128]{2,0,1:T(8,128)}), f32[528,8,128]{2,0,1:T(8,128)}, u32[]{:S(2)}, u32[]{:S(2)}) async-start(f32[528,8,128]{2,0,1:T(8,128)} %copy_bitcast_fusion), calls=%async_computation | async-start | bytes 4325376 | tf_op jit(solution)/shard_map/all_to_all | solution.py:49
  17.7 0.0 all-reduce.2.cloned.1.call-start
  17.7 0.6 multiply_reduce_fusion
  19.1 0.0 copy-done.2
  19.1 0.1 fusion.25
  19.2 0.0 copy-done.3
  19.2 0.6 cosine_multiply_fusion
  19.9 47.6 %all-to-all-done = f32[528,8,128]{2,0,1:T(8,128)} async-done(((f32[528,8,128]{2,0,1:T(8,128)}), f32[528,8,128]{2,0,1:T(8,128)}, u32[]{:S(2)}, u32[]{:S(2)}) %all-to-all-start) | async-done | bytes 2162720 | tf_op jit(solution)/shard_map/all_to_all | solution.py:49
  67.4 29.4 %gather_fusion = f32[8192,128]{1,0:T(8,128)} fusion(f32[4224,128]{1,0:T(8,128)} %bitcast.3, s32[8192]{0:T(1024)S(1)} %broadcast_clamp_fusion), kind=kCustom, calls=%fused_computation | custom fusion | bytes 8421376 | tf_op jit(solution)/shard_map/gather | solution.py:25
  96.8 5.6 %fusion.16 = f32[256,32,128]{2,0,1:T(8,128)S(1)} fusion(f32[32,256,128]{2,1,0:T(8,128)} %bitcast.23, f32[128,256]{1,0:T(8,128)S(1)} %get-tuple-element.8, f32[128,256]{1,0:T(8,128)S(1)} %get-tuple-element.7), kind=kOutput, calls=%fused_computation.17 | convolution fusion | flops 3221291008 | bytes 8650752 | tf_op jit(solution)/shard_map/kt,btp->kbp/dot_general | solution.py:26
  102.4 0.7 fusion.29
  103.1 0.0 copy-start.1
  103.1 5.7 %fusion.4 = f32[128,32,32]{2,1,0:T(8,128)} fusion(f32[128,32,128]{2,0,1:T(8,128)S(1)} %get-tuple-element.6), kind=kOutput, calls=%fused_computation.9 | convolution fusion | flops 201326592 | bytes 2621440 | tf_op jit(solution)/shard_map/fbp,fcp->fbc/dot_general | solution.py:34
  108.8 5.7 %fusion = f32[128,32,32]{2,1,0:T(8,128)S(1)} fusion(f32[128,32,128]{2,0,1:T(8,128)S(1)} %get-tuple-element.6, f32[128,32,128]{2,0,1:T(8,128)S(1)} %get-tuple-element.4), kind=kOutput, calls=%fused_computation.5 | convolution fusion | flops 201326592 | bytes 4718592 | tf_op jit(solution)/shard_map/fbp,fcp->fbc/dot_general | solution.py:37
  114.5 0.0 copy-done.1
  114.5 7.2 %subtract_bitcast_fusion = f32[1,128,32,32]{3,2,1,0:T(8,128)} fusion(f32[128,32,32]{2,1,0:T(8,128)S(1)} %fusion, f32[128,32,128]{2,0,1:T(8,128)S(1)} %get-tuple-element.6, f32[128,32,128]{2,0,1:T(8,128)S(1)} %get-tuple-element.4), kind=kOutput, calls=%fused_computation.2 | convolution fusion | flops 201457664 | bytes 5242880 | tf_op jit(solution)/shard_map/fbp,fcp->fbc/dot_general | solution.py:37
  121.7 2.7 copy.33
  124.3 9.7 %add_bitcast_fusion = f32[1,128,32,32]{3,2,1,0:T(8,128)} fusion(f32[128,32,32]{2,1,0:T(8,128)} %fusion.4, f32[128,32,128]{2,0,1:T(8,128)} %copy-done.1), kind=kOutput, calls=%fused_computation.3 | convolution fusion | flops 201457664 | bytes 3145728 | tf_op jit(solution)/shard_map/fbp,fcp->fbc/dot_general | solution.py:34
  134.1 2.7 copy.32
  136.7 1.1 maximum_multiply_fusion
  137.8 0.0 all-reduce.2.cloned.1.call-update
  137.9 0.6 broadcast_multiply_fusion
  138.5 128.4 %all-reduce.2.cloned.1.call-done = f32[2,128,32,32]{1,3,2,0:T(8,128)} async-done(((f32[2,128,32,32]{1,3,2,0:T(8,128)}), f32[2,128,32,32]{1,3,2,0:T(8,128)}) %all-reduce.2.cloned.1.call-update) | async-done | bytes 1048592 | tf_op jit(solution)/shard_map/psum | solution.py:56
  266.9 1.6 constant_dynamic-slice_fusion
  268.5 1.2 copy.34
  (3 shorter events, 0.1 us)
Async XLA Ops:
  7.2 1.6 copy-start
  10.3 8.8 %copy-start.2 = (s32[32]{0:T(128)S(1)}, s32[32]{0:T(128)}, u32[]{:S(2)}) copy-start(s32[32]{0:T(128)} %param.4) | copy-start | bytes 388
  10.3 9.0 %copy-start.3 = (s32[128]{0:T(128)S(1)}, s32[128]{0:T(128)}, u32[]{:S(2)}) copy-start(s32[128]{0:T(128)} %param.5) | copy-start | bytes 1540
  10.3 57.1 %all-to-all-start = ((f32[528,8,128]{2,0,1:T(8,128)}), f32[528,8,128]{2,0,1:T(8,128)}, u32[]{:S(2)}, u32[]{:S(2)}) async-start(f32[528,8,128]{2,0,1:T(8,128)} %copy_bitcast_fusion), calls=%async_computation | async-start | bytes 4325376 | tf_op jit(solution)/shard_map/all_to_all | solution.py:49
  17.7 249.3 %all-reduce.2.cloned.1.call-start = ((), (), s32[]{:S(2)}) async-start(), calls=%async_computation.1 | async-start | bytes 2097152 | tf_op jit(solution)/shard_map/psum | solution.py:56
  103.1 11.4 %copy-start.1 = (f32[128,32,128]{2,0,1:T(8,128)}, f32[128,32,128]{2,0,1:T(8,128)S(1)}, u32[]{:S(2)}) copy-start(f32[128,32,128]{2,0,1:T(8,128)S(1)} %get-tuple-element.4) | copy-start | bytes 6291460
Sparse Core Ops, SparseCore 0:
  138.0 128.9 all-reduce.1
where the time goes:
time: 277 us
  waiting for transfers between devices  176 us (64%)
  local copies, waits for them, and re-layouts  40.6 us (15%)
  matrix products  33.9 us (12%)
  between operations  14.8 us (5%)
  starting transfers between devices  7.42 us (3%)
  other arithmetic  3.87 us (1%)
    psum x1, waiting for transfers between devices, body(): summed = lax.psum(own_gram, ('tm', 'space'))  128 us
    all_to_all x1, waiting for transfers between devices, body(): lax.all_to_all(arranged, 'tm', split_axis=1, concat_axis=0, tiled=True)  47.6 us
    gather x1, local copies, waits for them, and re-layouts, block_spectra(): blocks = series[offsets]  29.4 us
    dot_general x1, matrix products, local_terms(): jnp.einsum('fbp,fcp->fbc', real_part, real_part, precision=highest)  9.72 us
    all_to_all x1, starting transfers between devices, body(): lax.all_to_all(arranged, 'tm', split_axis=1, concat_axis=0, tiled=True)  7.38 us
    dot_general x1, matrix products, local_terms(): jnp.einsum('fbp,fcp->fbc', real_part, imag_part, precision=highest)  7.21 us
    dot_general x1, matrix products, local_terms(): jnp.einsum('fbp,fcp->fbc', imag_part, imag_part, precision=highest)  5.68 us
    dot_general x1, matrix products, local_terms(): jnp.einsum('fbp,fcp->fbc', imag_part, real_part, precision=highest)  5.67 us
  transfers between devices with their start and end apart: 2, of which 2 were waited for; matrix products, arithmetic and copies ran while one was open for 1% of the time, Pallas kernels for 0%

commit v1 on v0

--- a/solution.py
+++ b/solution.py
@@ -7,6 +7,29 @@
 NFFT = 256
 NF = 128
 NB = 32
+
+
+def split_up(x, dim, peers):
+    dims = x.shape
+    blocks = x.reshape(*dims[:dim], peers, dims[dim] // peers, *dims[dim + 1 :])
+    return jnp.moveaxis(blocks, dim, 0)
+
+
+def in_order(tiles, dim):
+    dims = list(tiles.shape[1:])
+    dims[dim] *= tiles.shape[0]
+    return jnp.moveaxis(tiles, 0, dim).reshape(dims)
+
+
+def sent_to_each(x, axis, split_dim, concat_dim):
+    length, index = (lax.axis_size(axis), lax.axis_index(axis))
+    blocks = split_up(x, split_dim, length)
+    done = [blocks[index]]
+    for step in range(1, length):
+        sent = blocks[(index + step) % length]
+        done.append(lax.ppermute(sent, axis, [(i, (i + step) % length) for i in range(length)]))
+    blocks = jnp.stack(done)[(index - jnp.arange(length)) % length]
+    return in_order(blocks, concat_dim)
 
 
 def spectral_table(freq_lines):
@@ -45,11 +68,7 @@
     columns = snapshots.shape[1] // groups
     table = spectral_table(freq_lines)
     arranged = snapshots.reshape(snapshots.shape[0], groups, columns)
-    spectra = block_spectra(
-        lax.all_to_all(arranged, "tm", split_axis=1, concat_axis=0, tiled=True)[:, 0, :],
-        starts,
-        table,
-    )
+    spectra = block_spectra(sent_to_each(arranged, "tm", 1, 0)[:, 0, :], starts, table)
     total_points = columns * groups * lax.axis_size("space")
     power_density, own_gram = local_terms(spectra, 1.0 / (NB * total_points))
     per_device = NF // groups

time: 277 us -> 280 us (1.011)
  starting transfers between devices: 7.42 us -> 17.4 us
  waiting for transfers between devices: 176 us -> 168 us
  local copies, waits for them, and re-layouts: 40.6 us -> 44.3 us
    all_to_all x1 -> x0, waiting for transfers between devices: 47.6 us -> none  [body(): lax.all_to_all(arranged, 'tm', split_axis=1, concat_axis=0, tiled=True)]
    ppermute x0 -> x7, waiting for transfers between devices: none -> 32.5 us  [sent_to_each(): lax.ppermute(sent, axis, [(i, (i + step) % length) for i in range(length)])]
    ppermute x0 -> x7, starting transfers between devices: none -> 17.4 us  [sent_to_each(): lax.ppermute(sent, axis, [(i, (i + step) % length) for i in range(length)])]
    all_to_all x1 -> x0, starting transfers between devices: 7.38 us -> none  [body(): lax.all_to_all(arranged, 'tm', split_axis=1, concat_axis=0, tiled=True)]
    psum x1, waiting for transfers between devices: 128 us -> 135 us  [body(): summed = lax.psum(own_gram, ('tm', 'space'))]
  transfers between devices with their start and end apart: 2 -> 8, of which waited for: 2 -> 3; matrix products, arithmetic and copies ran while one was open for 1% -> 1% of each run, Pallas kernels for 0% -> 0%
where the time goes in v1:
time: 280 us
  waiting for transfers between devices  168 us (60%)
  local copies, waits for them, and re-layouts  44.3 us (16%)
  matrix products  31.6 us (11%)
  starting transfers between devices  17.4 us (6%)
  between operations  15 us (5%)
  other arithmetic  3.9 us (1%)
    psum x1, waiting for transfers between devices, body(): summed = lax.psum(own_gram, ('tm', 'space'))  135 us
    ppermute x7, waiting for transfers between devices, sent_to_each(): lax.ppermute(sent, axis, [(i, (i + step) % length) for i in range(length)])  32.5 us
    gather x1, local copies, waits for them, and re-layouts, block_spectra(): blocks = series[offsets]  27.9 us
    ppermute x7, starting transfers between devices, sent_to_each(): lax.ppermute(sent, axis, [(i, (i + step) % length) for i in range(length)])  17.4 us
    dot_general x1, matrix products, local_terms(): jnp.einsum('fbp,fcp->fbc', real_part, real_part, precision=highest)  7.39 us
    dot_general x1, matrix products, local_terms(): jnp.einsum('fbp,fcp->fbc', real_part, imag_part, precision=highest)  7.21 us
    dot_general x1, matrix products, local_terms(): jnp.einsum('fbp,fcp->fbc', imag_part, imag_part, precision=highest)  5.72 us
    dot_general x1, matrix products, local_terms(): jnp.einsum('fbp,fcp->fbc', imag_part, real_part, precision=highest)  5.67 us
  transfers between devices with their start and end apart: 8, of which 3 were waited for; matrix products, arithmetic and copies ran while one was open for 1% of the time, Pallas kernels for 0%

profile of v1, /device:TPU:0, one launch (start us, length us, event | category | flops | bytes accessed | tf_op | source)
XLA Modules:
  0.0 279.7 jit_solution(622454791731893518)
XLA Ops:
  7.2 0.0 all-reduce.2.cloned.1.call-start
  7.3 2.1 copy.32
  9.4 0.0 copy-start.1
  9.5 0.0 copy-start.2
  9.5 2.4 constant_dynamic-slice_fusion.1
  11.9 5.0 %collective-permute-start.5 = (f32[528,1,128]{2,0,1:T(8,128)S(1)}, f32[528,1,128]{2,0,1:T(8,128)S(1)}, u32[]{:S(2)}, u32[]{:S(2)}) collective-permute-start(f32[528,1,128]{2,0,1:T(8,128)S(1)} %bitcast.50), channel_id=1, source_target_pairs={{0,24},{4,28},{8,0},{12,4},{16,8},{20,12},{24,16},{28,20},{1,25},{... | collective-permute-start | bytes 811016 | tf_op jit(solution)/shard_map/ppermute | solution.py:30
  16.9 1.4 collective-permute-start.6
  18.3 0.0 collective-permute-start.4
  18.3 1.6 collective-permute-start.1
  19.9 1.9 collective-permute-start
  21.8 0.6 multiply_reduce_fusion
  23.2 0.0 copy-done.1
  23.2 0.1 fusion.25
  23.3 0.0 copy-done.2
  23.3 0.6 cosine_multiply_fusion
  24.0 17.9 %collective-permute-done = f32[528,1,128]{2,0,1:T(8,128)S(1)} collective-permute-done((f32[528,1,128]{2,0,1:T(8,128)}, f32[528,1,128]{2,0,1:T(8,128)S(1)}, u32[]{:S(2)}, u32[]{:S(2)}) %collective-permute-start) | collective-permute-done | bytes 270368 | tf_op jit(solution)/shard_map/ppermute | solution.py:30
  41.9 0.7 collective-permute-start.2
  42.5 0.0 collective-permute-done.1
  42.5 6.8 %collective-permute-start.3 = (f32[528,1,128]{2,0,1:T(8,128)}, f32[528,1,128]{2,0,1:T(8,128)S(1)}, u32[]{:S(2)}, u32[]{:S(2)}) collective-permute-start(f32[528,1,128]{2,0,1:T(8,128)} %bitcast.52), channel_id=1, source_target_pairs={{0,16},{4,20},{8,24},{12,28},{16,0},{20,4},{24,8},{28,12},{1,17},{... | collective-permute-start | bytes 811016 | tf_op jit(solution)/shard_map/ppermute | solution.py:30
  49.4 14.6 %collective-permute-done.2 = f32[528,1,128]{2,0,1:T(8,128)S(1)} collective-permute-done((f32[528,1,128]{2,0,1:T(8,128)}, f32[528,1,128]{2,0,1:T(8,128)S(1)}, u32[]{:S(2)}, u32[]{:S(2)}) %collective-permute-start.2) | collective-permute-done | bytes 270368 | tf_op jit(solution)/shard_map/ppermute | solution.py:30
  64.0 0.0 collective-permute-done.3
  64.1 0.0 collective-permute-done.4
  64.1 0.0 collective-permute-done.5
  64.2 0.0 collective-permute-done.6
  64.2 0.0 copy-start
  64.2 1.3 copy-done
  65.5 2.3 gather_fusion
  67.8 27.9 %gather_fusion.1 = f32[8192,128]{1,0:T(8,128)} fusion(f32[4224,128]{1,0:T(8,128)S(1)} %bitcast.43, s32[8192]{0:T(1024)S(1)} %broadcast_clamp_fusion), kind=kCustom, calls=%fused_computation.1 | custom fusion | bytes 8421376 | tf_op jit(solution)/shard_map/gather | solution.py:48
  95.7 5.6 %fusion.16 = f32[256,32,128]{2,0,1:T(8,128)S(1)} fusion(f32[32,256,128]{2,1,0:T(8,128)} %bitcast.44, f32[128,256]{1,0:T(8,128)S(1)} %get-tuple-element.16, f32[128,256]{1,0:T(8,128)S(1)} %get-tuple-element.15), kind=kOutput, calls=%fused_computation.24 | convolution fusion | flops 3221291008 | bytes 8650752 | tf_op jit(solution)/shard_map/kt,btp->kbp/dot_general | solution.py:49
  101.3 0.7 fusion.31
  102.1 5.7 %fusion.4 = f32[128,32,32]{2,1,0:T(8,128)} fusion(f32[128,32,128]{2,0,1:T(8,128)S(1)} %get-tuple-element.6), kind=kOutput, calls=%fused_computation.9 | convolution fusion | flops 201326592 | bytes 2621440 | tf_op jit(solution)/shard_map/fbp,fcp->fbc/dot_general | solution.py:57
  107.8 5.7 %fusion = f32[128,32,32]{2,1,0:T(8,128)S(1)} fusion(f32[128,32,128]{2,0,1:T(8,128)S(1)} %get-tuple-element.6, f32[128,32,128]{2,0,1:T(8,128)S(1)} %get-tuple-element.4), kind=kOutput, calls=%fused_computation.5 | convolution fusion | flops 201326592 | bytes 4718592 | tf_op jit(solution)/shard_map/fbp,fcp->fbc/dot_general | solution.py:60
  113.5 7.2 %subtract_bitcast_fusion = f32[1,128,32,32]{3,2,1,0:T(8,128)} fusion(f32[128,32,32]{2,1,0:T(8,128)S(1)} %fusion, f32[128,32,128]{2,0,1:T(8,128)S(1)} %get-tuple-element.6, f32[128,32,128]{2,0,1:T(8,128)S(1)} %get-tuple-element.4), kind=kOutput, calls=%fused_computation.2 | convolution fusion | flops 201457664 | bytes 5242880 | tf_op jit(solution)/shard_map/fbp,fcp->fbc/dot_general | solution.py:60
  120.7 2.7 copy.30
  123.3 7.4 %add_bitcast_fusion = f32[1,128,32,32]{3,2,1,0:T(8,128)} fusion(f32[128,32,32]{2,1,0:T(8,128)} %fusion.4, f32[128,32,128]{2,0,1:T(8,128)S(1)} %get-tuple-element.4), kind=kOutput, calls=%fused_computation.3 | convolution fusion | flops 201457664 | bytes 3145728 | tf_op jit(solution)/shard_map/fbp,fcp->fbc/dot_general | solution.py:57
  130.7 2.7 copy.29
  133.4 1.1 maximum_multiply_fusion
  134.5 0.0 all-reduce.2.cloned.1.call-update
  134.5 0.6 broadcast_multiply_fusion
  135.2 135.0 %all-reduce.2.cloned.1.call-done = f32[2,128,32,32]{1,3,2,0:T(8,128)} async-done(((f32[2,128,32,32]{1,3,2,0:T(8,128)}), f32[2,128,32,32]{1,3,2,0:T(8,128)}) %all-reduce.2.cloned.1.call-update) | async-done | bytes 1048592 | tf_op jit(solution)/shard_map/psum | solution.py:75
  270.1 1.6 constant_dynamic-slice_fusion
  271.7 1.2 copy.31
  (13 shorter events, 0.3 us)
Async XLA Ops:
  7.2 263.0 %all-reduce.2.cloned.1.call-start = ((), (), s32[]{:S(2)}) async-start(), calls=%async_computation | async-start | bytes 2097152 | tf_op jit(solution)/shard_map/psum | solution.py:75
  9.4 13.7 %copy-start.1 = (s32[32]{0:T(128)S(1)}, s32[32]{0:T(128)}, u32[]{:S(2)}) copy-start(s32[32]{0:T(128)} %param.4) | copy-start | bytes 388
  9.5 13.8 %copy-start.2 = (s32[128]{0:T(128)S(1)}, s32[128]{0:T(128)}, u32[]{:S(2)}) copy-start(s32[128]{0:T(128)} %param.5) | copy-start | bytes 1540
  11.9 52.3 %collective-permute-start.5 = (f32[528,1,128]{2,0,1:T(8,128)S(1)}, f32[528,1,128]{2,0,1:T(8,128)S(1)}, u32[]{:S(2)}, u32[]{:S(2)}) collective-permute-start(f32[528,1,128]{2,0,1:T(8,128)S(1)} %bitcast.50), channel_id=1, source_target_pairs={{0,24},{4,28},{8,0},{12,4},{16,8},{20,12},{24,16},{28,20},{1,25},{... | collective-permute-start | bytes 811016 | tf_op jit(solution)/shard_map/ppermute | solution.py:30
  16.9 47.3 %collective-permute-start.6 = (f32[528,1,128]{2,0,1:T(8,128)S(1)}, f32[528,1,128]{2,0,1:T(8,128)S(1)}, u32[]{:S(2)}, u32[]{:S(2)}) collective-permute-start(f32[528,1,128]{2,0,1:T(8,128)S(1)} %bitcast.49), channel_id=1, source_target_pairs={{0,28},{4,0},{8,4},{12,8},{16,12},{20,16},{24,20},{28,24},{1,29},{... | collective-permute-start | bytes 811016 | tf_op jit(solution)/shard_map/ppermute | solution.py:30
  18.3 45.8 %collective-permute-start.4 = (f32[528,1,128]{2,0,1:T(8,128)S(1)}, f32[528,1,128]{2,0,1:T(8,128)S(1)}, u32[]{:S(2)}, u32[]{:S(2)}) collective-permute-start(f32[528,1,128]{2,0,1:T(8,128)S(1)} %bitcast.51), channel_id=1, source_target_pairs={{0,20},{4,24},{8,28},{12,0},{16,4},{20,8},{24,12},{28,16},{1,21},{... | collective-permute-start | bytes 811016 | tf_op jit(solution)/shard_map/ppermute | solution.py:30
  18.3 24.3 %collective-permute-start.1 = (f32[528,1,128]{2,0,1:T(8,128)}, f32[528,1,128]{2,0,1:T(8,128)S(1)}, u32[]{:S(2)}, u32[]{:S(2)}) collective-permute-start(f32[528,1,128]{2,0,1:T(8,128)} %bitcast.4), channel_id=1, source_target_pairs={{0,8},{4,12},{8,16},{12,20},{16,24},{20,28},{24,0},{28,4},{1,9},{5... | collective-permute-start | bytes 811016 | tf_op jit(solution)/shard_map/ppermute | solution.py:30
  19.9 22.0 %collective-permute-start = (f32[528,1,128]{2,0,1:T(8,128)}, f32[528,1,128]{2,0,1:T(8,128)S(1)}, u32[]{:S(2)}, u32[]{:S(2)}) collective-permute-start(f32[528,1,128]{2,0,1:T(8,128)} %bitcast.2), channel_id=1, source_target_pairs={{0,4},{4,8},{8,12},{12,16},{16,20},{20,24},{24,28},{28,0},{1,5},{5... | collective-permute-start | bytes 811016 | tf_op jit(solution)/shard_map/ppermute | solution.py:30
  41.9 22.2 %collective-permute-start.2 = (f32[528,1,128]{2,0,1:T(8,128)}, f32[528,1,128]{2,0,1:T(8,128)S(1)}, u32[]{:S(2)}, u32[]{:S(2)}) collective-permute-start(f32[528,1,128]{2,0,1:T(8,128)} %bitcast.53), channel_id=1, source_target_pairs={{0,12},{4,16},{8,20},{12,24},{16,28},{20,0},{24,4},{28,8},{1,13},{... | collective-permute-start | bytes 811016 | tf_op jit(solution)/shard_map/ppermute | solution.py:30
  42.5 21.5 %collective-permute-start.3 = (f32[528,1,128]{2,0,1:T(8,128)}, f32[528,1,128]{2,0,1:T(8,128)S(1)}, u32[]{:S(2)}, u32[]{:S(2)}) collective-permute-start(f32[528,1,128]{2,0,1:T(8,128)} %bitcast.52), channel_id=1, source_target_pairs={{0,16},{4,20},{8,24},{12,28},{16,0},{20,4},{24,8},{28,12},{1,17},{... | collective-permute-start | bytes 811016 | tf_op jit(solution)/shard_map/ppermute | solution.py:30
  64.2 1.4 copy-start
Sparse Core Ops, SparseCore 0:
  134.6 135.4 all-reduce.1
